TPU v7x, 32 devices: a whole 2x2x4 slice. The times are simulated.
32 devices in a mesh: ka: 2 (over x), pts: 16 (over z, y, core).
Axes of the slice: x: 2, y: 2, z: 4, core: 2. Of those that a mesh axis runs over, the one named last changes fastest.
Arguments:
- orbitals: bfloat16 [216, 2, 4096, 384], P('ka', None, 'pts'), may hold values from -1.5 to 1.5
- counts: int32 [216], P('ka'), may hold values from 60 to 300
- occupation: float32 [216, 384], P('ka'), may hold values from 0.2 to 1
- coulomb: bfloat16 [216, 2, 16, 4096], P('ka', None, None, 'pts'), may hold values from -24 to 24
Outputs:
- exchange_block: bfloat16 [216, 2, 16, 4096], P('ka', None, None, 'pts')
Inputs may be any that keep to these rules, and one draw needn't show every extreme that they name: `counts`: between 60 and 300 occupied bands per k-point.
All inputs are finite; a program needn't handle non-finite values.
Results may differ from a plain program's by a relative error of at most 0.0057.
Values may be sent and summed in bfloat16 or wider, within the bound.
No kernel may reach another device: no remote copies, remote signals or barrier semaphores. Data moves between devices by JAX's collectives and lax.ppermute only.
A program may use at most 128 MiB of HBM per device.

v0:
```python
import jax
import jax.numpy as jnp
from jax import lax
from jax.experimental import pallas as pl
from jax.experimental.pallas import tpu as pltpu
from jax.sharding import PartitionSpec as P


KSIDE = 6
ROW_DEV = 1
HALF = KSIDE // 2
LANES = 128
ROOT = 0.8660254037844386


LANE_HALF = LANES // 2
GROUP = 6
AHEAD = 2
BLOCK = 16


def band_order(counts, parts):
    tiles = -(-counts.reshape(parts, -1) // LANES)
    size = tiles.shape[1]
    index = jnp.arange(size, dtype=jnp.int32)
    key = tiles * size - index
    rank = jnp.sum((key[:, None, :] > key[:, :, None]).astype(jnp.int32), 2)
    hit = (rank[:, :, None] == index).astype(jnp.int32)
    return jnp.sum(hit * index[:, None], 1), jnp.sum(hit * tiles[:, :, None], 1)


def density_part(spread, order, tiles, parts, orbitals, start, count):
    rows = len(parts)
    width = parts[0].shape[1]
    columns, slots = orbitals.shape[2:]
    keep = rows // 2
    first = start // BLOCK * BLOCK
    span = -(-(start + count - first) // BLOCK) * BLOCK
    group = GROUP
    ahead = AHEAD
    groups = count // group
    ring = ahead + 1
    whole = (slots // LANES - 1) * LANES
    depth = slots // LANES
    splits = columns // LANES

    def kernel(order_ref, tiles_ref, spread_ref, *refs):
        sources, orb, refs = refs[:rows], refs[rows], refs[rows + 1 :]
        keep_ref, send_refs, (raw, left, buf, raw_sem, sem) = refs[0], refs[1 : 1 + splits], refs[1 + splits :]
        row_copies = [
            pltpu.make_async_copy(sources[i].at[pl.ds(first, span)], raw.at[i], raw_sem.at[i]) for i in range(rows)
        ]

        def per_class(g, act):
            for n in range(1, depth + 1):
                pl.when(tiles_ref[g * group] == n)(lambda n=n: act(n))

        def panels(g, n, act):
            lanes = pl.ds(0, n * LANES)
            for u in range(group):
                slot = g % ring * group + u
                source = orb.at[start + order_ref[g * group + u], :, :, lanes]
                act(pltpu.make_async_copy(source, buf.at[slot, :, :, lanes], sem.at[slot]))

        for copy in row_copies:
            copy.start()
        for g in range(min(ahead, groups)):
            per_class(g, lambda n, g=g: panels(g, n, lambda copy: copy.start()))
        for copy in row_copies:
            copy.wait()
        lane = lax.broadcasted_iota(jnp.int32, (BLOCK * rows, LANES), 1)
        for at in range(0, span, BLOCK):
            stacked = jnp.concatenate([raw[i, at : at + BLOCK, :] for i in range(rows)], 0)
            mixed = jnp.dot(spread_ref[...], stacked, preferred_element_type=jnp.float32)
            last = mixed[:, 2 * whole :]
            re_last = jnp.where(lane < LANE_HALF, last, 0.0)
            im_last = jnp.where(lane < LANE_HALF, pltpu.roll(last, LANE_HALF, 1), 0.0)
            pieces = [mixed[:, :whole], re_last, mixed[:, whole : 2 * whole], im_last]
            left[at * rows : (at + BLOCK) * rows, :] = jnp.concatenate(pieces, 1).astype(jnp.bfloat16)
        dims = (((1,), (1,)), ((), ()))
        skip = start - first

        def gram(g, n):
            panels(g, n, lambda copy: copy.wait())
            for u in range(group):
                k = order_ref[g * group + u]
                slot = g % ring * group + u
                row = pl.ds(pl.multiple_of((k + skip) * rows, rows), rows)
                re = left[row, : n * LANES]
                im = left[row, slots : slots + n * LANES]
                lhs = jnp.concatenate([jnp.concatenate([re, im], 1), jnp.concatenate([im, -re], 1)], 0)
                rhs = jnp.concatenate([buf[slot, 0, :, : n * LANES], buf[slot, 1, :, : n * LANES]], 1)
                out = lax.dot_general(lhs, rhs, dims, preferred_element_type=jnp.float32).astype(jnp.bfloat16)
                keep_ref[k, 0] = out[:keep]
                keep_ref[k, 1] = out[rows : rows + keep]
                for j in range(splits):
                    send_refs[j][k, 0] = out[keep:rows, j * LANES : (j + 1) * LANES]
                    send_refs[j][k, 1] = out[rows + keep :, j * LANES : (j + 1) * LANES]

        def step(g, _):
            @pl.when(g + ahead < groups)
            def _():
                per_class(g + ahead, lambda n: panels(g + ahead, n, lambda copy: copy.start()))

            per_class(g, lambda n: gram(g, n))
            return 0

        lax.fori_loop(0, groups, step, 0)

    anywhere = pl.BlockSpec(memory_space=pl.ANY)
    local = pl.BlockSpec(memory_space=pltpu.VMEM)
    scalars = pl.BlockSpec(memory_space=pltpu.SMEM)
    kept = jax.ShapeDtypeStruct((count, 2, keep, columns), jnp.bfloat16)
    sent = jax.ShapeDtypeStruct((count, 2, keep, LANES), jnp.bfloat16)
    return pl.pallas_call(
        kernel,
        out_shape=(kept,) + (sent,) * splits,
        in_specs=[scalars, scalars, local] + [anywhere] * (rows + 1),
        out_specs=(local,) * (1 + splits),
        scratch_shapes=[
            pltpu.VMEM((rows, span, width), jnp.bfloat16),
            pltpu.VMEM((span * rows, 2 * slots), jnp.bfloat16),
            pltpu.VMEM((ring * group, 2, columns, slots), jnp.bfloat16),
            pltpu.SemaphoreType.DMA((rows,)),
            pltpu.SemaphoreType.DMA((ring * group,)),
        ],
        name="density_part",
    )(order, tiles, spread, *parts, orbitals)


PIECES = 4


def take_rows(which, value, keep):
    count, _, _, columns = value.shape
    size = count // PIECES

    def kernel(which_ref, value_ref, out_ref, held, in_sem, out_sem):
        rows = pl.ds(pl.multiple_of(which_ref[0] * keep, keep), keep)

        def load(i):
            part = pl.ds(i * size, size)
            return pltpu.make_async_copy(value_ref.at[part, :, rows, :], held.at[part], in_sem.at[i])

        def store(i):
            part = pl.ds(i * size, size)
            return pltpu.make_async_copy(held.at[part], out_ref.at[part], out_sem.at[i])

        for i in range(PIECES):
            load(i).start()
        for i in range(PIECES):
            load(i).wait()
            store(i).start()
        for i in range(PIECES):
            store(i).wait()

    shape = (count, 2, keep, columns)
    anywhere = pl.BlockSpec(memory_space=pl.ANY)
    return pl.pallas_call(
        kernel,
        out_shape=jax.ShapeDtypeStruct(shape, value.dtype),
        in_specs=[pl.BlockSpec(memory_space=pltpu.SMEM), anywhere],
        out_specs=anywhere,
        scratch_shapes=[
            pltpu.VMEM(shape, value.dtype),
            pltpu.SemaphoreType.DMA((PIECES,)),
            pltpu.SemaphoreType.DMA((PIECES,)),
        ],
        name="take_rows",
    )(which, value)


def add(a, b):
    return a[0] + b[0], a[1] + b[1]


def sub(a, b):
    return a[0] - b[0], a[1] - b[1]


def three(a, b, c, inverse):
    total = add(b, c)
    first = add(a, total)
    middle = a[0] - 0.5 * total[0], a[1] - 0.5 * total[1]
    turn = ROOT * (b[0] - c[0]), ROOT * (b[1] - c[1])
    low = middle[0] + turn[1], middle[1] - turn[0]
    high = middle[0] - turn[1], middle[1] + turn[0]
    return (first, high, low) if inverse else (first, low, high)


def six(x):
    u = three(add(x[0], x[3]), add(x[4], x[1]), add(x[2], x[5]), False)
    v = three(sub(x[0], x[3]), sub(x[4], x[1]), sub(x[2], x[5]), False)
    return list(u) + list(v)


def six_back(x):
    u = three(*x[:3], True)
    v = three(*x[3:], True)
    return [add(u[0], v[0]), sub(u[1], v[1]), add(u[2], v[2]), sub(u[0], v[0]), add(u[1], v[1]), sub(u[2], v[2])]


def first_pass(own, other, work):
    def load(ref, k):
        return ref[k, 0].astype(jnp.float32), ref[k, 1].astype(jnp.float32)

    for kx in range(HALF):

        def body(ky, _):
            base = ky * KSIDE + kx * KSIDE * KSIDE * (1 if len(own) == 1 else 0)
            mine = [load(own[kx % len(own)], base + kz) for kz in range(KSIDE)]
            theirs = [load(other[kx % len(other)], base + kz) for kz in range(KSIDE)]
            plus = six([add(a, b) for a, b in zip(mine, theirs)])
            minus = six([sub(b, a) if kx % 2 else sub(a, b) for a, b in zip(mine, theirs)])
            for sign, values in enumerate((plus, minus)):
                for kz in range(KSIDE):
                    for part in range(2):
                        work[sign, kz, kx, ky, part] = values[kz][part]
            return 0

        lax.fori_loop(0, KSIDE, body, 0)


def plane_forward(work, sign, kz):
    grid = []
    for kx in range(HALF):
        grid.append(six([(work[sign, kz, kx, ky, 0], work[sign, kz, kx, ky, 1]) for ky in range(KSIDE)]))
    for ky in range(KSIDE):
        column = three(grid[0][ky], grid[1][ky], grid[2][ky], False)
        for kx in range(HALF):
            grid[kx][ky] = column[kx]
    return grid


def coulomb_transform(which, coulomb, other, column):
    count, _, rows, _ = other.shape
    scale = -0.5 / (HALF * HALF * HALF * 4 * KSIDE * KSIDE * KSIDE)

    def kernel(which_ref, own_ref, other_ref, out_ref, work):
        first_pass([own_ref], [other_ref], work)
        flip = jnp.where(which_ref[0] == 0, scale, -scale).astype(jnp.float32)

        def body(kz, _):
            for sign in range(2):
                factor = flip if sign else jnp.float32(scale)
                grid = plane_forward(work, sign, kz)
                for kx in range(HALF):
                    for ky in range(KSIDE):
                        for part in range(2):
                            out_ref[sign, kz, kx, ky, part] = grid[kx][ky][part] * factor
            return 0

        lax.fori_loop(0, KSIDE, body, 0)

    shape = (2, KSIDE, HALF, KSIDE, 2, rows, LANES)
    block = (count, 2, rows, LANES)
    return pl.pallas_call(
        kernel,
        out_shape=jax.ShapeDtypeStruct(shape, jnp.float32),
        grid_spec=pltpu.PrefetchScalarGridSpec(
            num_scalar_prefetch=1,
            grid=(1,),
            in_specs=[
                pl.BlockSpec(block, lambda i, w: (0, 0, w[0], column)),
                pl.BlockSpec(block, lambda i, w: (0, 0, 0, column)),
            ],
            out_specs=pl.BlockSpec(shape, lambda i, w: (0,) * 7),
            scratch_shapes=[pltpu.VMEM(shape, jnp.float32)],
        ),
        name="coulomb_transform",
    )(which, coulomb, other)


def convolve(which, own, other, kernel_hat, column, whole):
    planes = len(own)
    rows, columns = own[0].shape[2:]
    count = sum(value.shape[0] for value in own)

    def kernel(which_ref, *refs):
        own_refs, other_refs, hat = refs[:planes], refs[planes : 2 * planes], refs[2 * planes]
        keep_ref, send_ref, work = refs[-3:]
        first_pass(own_refs, other_refs, work)

        def middle(kz, _):
            for sign in range(2):
                grid = plane_forward(work, sign, kz)
                for ky in range(KSIDE):
                    column_values = []
                    for kx in range(HALF):
                        a, b = grid[kx][ky]
                        c, d = hat[sign, kz, kx, ky, 0], hat[sign, kz, kx, ky, 1]
                        column_values.append((a * c - b * d, a * d + b * c))
                    column_values = three(*column_values, True)
                    for kx in range(HALF):
                        grid[kx][ky] = column_values[kx]
                for kx in range(HALF):
                    values = six_back(grid[kx])
                    for ky in range(KSIDE):
                        for part in range(2):
                            work[sign, kz, kx, ky, part] = values[ky][part]
            return 0

        lax.fori_loop(0, KSIDE, middle, 0)

        def last(ky, _):
            for kx in range(HALF):
                both = []
                for sign in range(2):
                    both.append(six_back([(work[sign, kz, kx, ky, 0], work[sign, kz, kx, ky, 1]) for kz in range(KSIDE)]))
                base = (kx * KSIDE + ky) * KSIDE
                for kz in range(KSIDE):
                    for part in range(2):
                        plus, minus = both[0][kz][part], both[1][kz][part]
                        if kx % 2:
                            minus = -minus
                        keep_ref[base + kz, part] = (plus + minus).astype(jnp.bfloat16)
                        send_ref[base + kz, part] = (plus - minus).astype(jnp.bfloat16)
            return 0

        lax.fori_loop(0, KSIDE, last, 0)

    shape = (2, KSIDE, HALF, KSIDE, 2, rows, LANES)
    block = (count, 2, rows, LANES)
    plane = pl.BlockSpec((count // planes, 2, rows, LANES), lambda i, w: (0, 0, 0, column))
    come = pl.BlockSpec((count // planes, 2, rows, LANES), lambda i, w: (0, 0, 0, 0))
    specs = [plane] * planes + [come] * planes + [pl.BlockSpec(shape, lambda i, w: (0,) * 7)]
    extra = () if whole is None else (whole,)
    return pl.pallas_call(
        kernel,
        out_shape=(
            jax.ShapeDtypeStruct((count, 2, 2 * rows, columns), jnp.bfloat16),
            jax.ShapeDtypeStruct(block, jnp.bfloat16),
        ),
        grid_spec=pltpu.PrefetchScalarGridSpec(
            num_scalar_prefetch=1,
            grid=(1,),
            in_specs=specs + [pl.BlockSpec(memory_space=pl.ANY)] * len(extra),
            out_specs=(
                pl.BlockSpec(block, lambda i, w: (0, 0, w[0], column)),
                pl.BlockSpec(block, lambda i, w: (0, 0, 0, 0)),
            ),
            scratch_shapes=[pltpu.VMEM(shape, jnp.float32)],
        ),
        input_output_aliases={2 + 2 * planes: 0} if extra else {},
        name="convolve",
    )(which, *own, *other, kernel_hat, *extra)


def band_gram(left, right):

    def product(first, second):
        return jnp.einsum("krb,knb->krn", first, second, preferred_element_type=jnp.float32)

    real = product(left[:, 0], right[:, 0]) + product(left[:, 1], right[:, 1])
    imag = product(left[:, 1], right[:, 0]) - product(left[:, 0], right[:, 1])
    return jnp.stack([real, imag], 1)


def side_table(sign):
    index = jnp.arange(KSIDE, dtype=jnp.int32)
    phase = index[:, None] * index[None, :] % KSIDE
    angle = phase.astype(jnp.float32) * (2.0 * jnp.pi / KSIDE)
    cosine = jnp.cos(angle)
    sine = jnp.sin(angle) * sign
    top = jnp.stack([cosine, sine], 2)
    bottom = jnp.stack([-sine, cosine], 2)
    return jnp.stack([top, bottom], 1)


def mesh_transform(values, sign):
    table = side_table(sign)
    forms = ["acbd,bxydm->axycm", "acbd,xbydm->xaycm", "acbd,xybdm->xyacm"]
    for form in forms:
        values = jnp.einsum(
            form, table, values, precision=lax.Precision.HIGHEST, preferred_element_type=jnp.float32
        )
    return values


def convolve_any(density, kernel):
    shape = density.shape
    count = shape[0]
    dens = mesh_transform(density.astype(jnp.float32).reshape(KSIDE, KSIDE, KSIDE, 2, -1), 1.0)
    kern = mesh_transform(kernel.astype(jnp.float32).reshape(KSIDE, KSIDE, KSIDE, 2, -1), 1.0)
    prod_re = kern[:, :, :, 0] * dens[:, :, :, 0] - kern[:, :, :, 1] * dens[:, :, :, 1]
    prod_im = kern[:, :, :, 0] * dens[:, :, :, 1] + kern[:, :, :, 1] * dens[:, :, :, 0]
    back = mesh_transform(jnp.stack([prod_re, prod_im], 3), -1.0)
    scale = -1.0 / (count * count)
    return (back * scale).reshape(shape).astype(jnp.bfloat16)


def slab_rows(orbitals, counts, occupation):
    slots = orbitals.shape[3]
    band = jnp.arange(slots, dtype=jnp.int32)
    weights = jnp.where(band[None, :] < counts[:, None], occupation, jnp.float32(0.0))
    return (orbitals[:, :, :ROW_DEV, :].astype(jnp.float32) * weights[:, None, None, :]).astype(
        jnp.bfloat16
    )


def local_any(orbitals, counts, occupation, coulomb):
    weighted = slab_rows(orbitals, counts, occupation)
    gathered = lax.all_gather(weighted, "pts", axis=2, tiled=True)
    density = band_gram(gathered, orbitals).astype(jnp.bfloat16)
    result = convolve_any(
        lax.all_to_all(density, "ka", split_axis=3, concat_axis=0, tiled=True),
        lax.all_to_all(coulomb, "ka", split_axis=3, concat_axis=0, tiled=True),
    )
    return lax.all_to_all(result, "ka", split_axis=0, concat_axis=3, tiled=True)


def gather_rows(block, ring):
    def move(value, dest):
        pairs = []
        for z in range(ring):
            for y in range(2):
                for core in range(2):
                    to_z, to_y, to_core = dest(z, y, core)
                    pairs.append(((z * 2 + y) * 2 + core, (to_z % ring * 2 + to_y) * 2 + to_core))
        return lax.ppermute(value, "pts", pairs)

    def twin(z, y, core):
        return z, y, 1 - core

    def along(z, y, core):
        return z + 1 - 2 * core, y, core

    def across(z, y, core):
        return z, 1 - y, core

    def corner(z, y, core):
        return z + 1 - 2 * core, 1 - y, core

    here = lax.axis_index("pts")
    core = here % 2
    y = here // 2 % 2
    z = here // 4

    def index(dz, flip_y, of_core):
        return ((z + dz) % ring * 2 + (1 - y if flip_y else y)) * 2 + of_core

    back = 2 * core - 1
    near = move(block, twin)
    side_own = move(block, along)
    corner_own = move(block, corner)
    across_own = move(block, across)
    side_twin = move(near, along)
    corner_twin = move(near, corner)
    far = move(side_own, along)
    far_corner = move(corner_own, along)
    received = [
        (side_own, back, 0, core),
        (side_twin, back, 0, 1 - core),
        (corner_own, back, 1, core),
        (corner_twin, back, 1, 1 - core),
        (across_own, 0, 1, core),
        (far, 2 * back, 0, core),
        (far_corner, 2 * back, 1, core),
    ]
    parts = [block, near]
    where = [index(0, 0, core), index(0, 0, 1 - core)]
    for value, dz, flip_y, of_core in received:
        parts.append(value)
        where.append(index(dz, flip_y, of_core))
        parts.append(move(value, twin))
        where.append(index(-dz, flip_y, 1 - of_core))
    return parts, jnp.stack(where)


def pack_block(weighted):
    count, _, _, slots = weighted.shape
    whole = slots - LANES
    re, im = weighted[:, 0, 0], weighted[:, 1, 0]
    middle = whole + LANE_HALF
    block = jnp.concatenate([re[:, :whole], im[:, :whole], re[:, whole:middle], im[:, whole:middle]], 1)
    return jnp.pad(block, ((0, -count % BLOCK), (0, 0)))


def local_pair(orbitals, counts, occupation, coulomb):
    swap = [(0, 1), (1, 0)]
    count, _, columns, _ = orbitals.shape
    rows = coulomb.shape[2]
    keep = rows // 2
    half = lax.axis_index("ka")
    mine = half.astype(jnp.int32).reshape(1)
    theirs = 1 - mine
    other_coulomb = lax.ppermute(take_rows(theirs, coulomb, keep), "ka", swap)
    block = pack_block(slab_rows(orbitals, counts, occupation))
    parts, where = gather_rows(block, lax.axis_size("pts") // 4)
    where = ((where + keep * half) % rows).astype(jnp.int32)
    place = jnp.arange(rows * BLOCK, dtype=jnp.int32)
    target = jnp.broadcast_to(where[:, None], (rows, BLOCK)).reshape(-1)
    spread = (place[:, None] // rows == place[None, :] % BLOCK) & (place[:, None] % rows == target[None, :])
    spread = spread.astype(jnp.bfloat16)
    splits = columns // LANES
    order, tiles = band_order(counts, HALF)
    order, tiles, spread = lax.optimization_barrier((order, tiles, spread))
    size = count // HALF
    own, other = [], []
    for i in range(HALF):
        kept, *sent = density_part(spread, order[i], tiles[i], parts, orbitals, i * size, size)
        own.append(kept)
        other.append([])
        for value in sent:
            other[i].append(lax.ppermute(value, "ka", swap))
    whole = None
    returned = []
    for j in range(splits):
        hat = coulomb_transform(mine, coulomb, other_coulomb, j)
        whole, sent = convolve(mine, own, [value[j] for value in other], hat, j, whole)
        returned.append(lax.ppermute(sent, "ka", swap))
    for j, value in enumerate(returned):
        whole = lax.dynamic_update_slice(whole, value, (0, 0, theirs[0] * keep, j * LANES))
    return whole


def solution(mesh):
    pair = mesh.shape["ka"] == 2 and mesh.shape["pts"] == BLOCK

    def local(orbitals, counts, occupation, coulomb):
        columns = orbitals.shape[2]
        if pair and columns % LANES == 0 and orbitals.shape[0] % (HALF * KSIDE * KSIDE) == 0:
            return local_pair(orbitals, counts, occupation, coulomb)
        return local_any(orbitals, counts, occupation, coulomb)

    return jax.shard_map(
        local,
        mesh=mesh,
        in_specs=(P("ka", None, "pts", None), P("ka"), P("ka", None), P("ka", None, None, "pts")),
        out_specs=P("ka", None, None, "pts"),
        check_vma=False,
    )
```

profile of v0, /device:TPU:0, one launch (start us, length us, event | category | flops | bytes accessed | tf_op | source)
XLA Modules:
  0.0 98.4 jit_solution(12096651385850694852)
XLA Ops:
  0.0 1.5 %slice.41 = bf16[108,2,1,384]{3,2,1,0:T(2,128)(2,1)S(1)} slice(bf16[108,2,256,384]{3,2,1,0:T(8,128)(2,1)} %refs_16_.5), slice={[0:108], [0:2], [0:1], [0:384]} | slice | bytes 331776 | tf_op jit(solution)/shard_map/slice | solution.py:396
  2.7 3.1 %collective-permute-start.9 = (bf16[112,640]{1,0:T(8,128)(2,1)S(1)}, bf16[112,640]{1,0:T(8,128)(2,1)S(1)}, u32[]{:S(2)}, u32[]{:S(2)}) collective-permute-start(bf16[112,640]{1,0:T(8,128)(2,1)S(1)} %fusion.7.refs_0_), channel_id=1, source_target_pairs={{0,2},{1,3},{2,0},{3,1},{4,6},{5,7},{6,4},{7,5},{8,10},{9,11},{10,... | collective-permute-start | bytes 430088 | tf_op jit(solution)/shard_map/ppermute | solution.py:420
  5.8 1.5 %collective-permute-start.5 = (bf16[112,640]{1,0:T(8,128)(2,1)S(1)}, bf16[112,640]{1,0:T(8,128)(2,1)S(1)}, u32[]{:S(2)}, u32[]{:S(2)}) collective-permute-start(bf16[112,640]{1,0:T(8,128)(2,1)S(1)} %fusion.7.refs_0_), channel_id=1, source_target_pairs={{0,6},{1,15},{2,4},{3,13},{4,10},{5,3},{6,8},{7,1},{8,14},{9,7},{1... | collective-permute-start | bytes 430088 | tf_op jit(solution)/shard_map/ppermute | solution.py:420
  7.3 1.6 %collective-permute-start.1 = (bf16[112,640]{1,0:T(8,128)(2,1)S(1)}, bf16[112,640]{1,0:T(8,128)(2,1)S(1)}, u32[]{:S(2)}, u32[]{:S(2)}) collective-permute-start(bf16[112,640]{1,0:T(8,128)(2,1)S(1)} %fusion.7.refs_0_), channel_id=1, source_target_pairs={{0,4},{1,13},{2,6},{3,15},{4,8},{5,1},{6,10},{7,3},{8,12},{9,5},{1... | collective-permute-start | bytes 430088 | tf_op jit(solution)/shard_map/ppermute | solution.py:420
  8.9 2.0 %take_rows.1 = bf16[108,2,8,256]{3,2,1,0:T(8,128)(2,1)} custom-call(s32[1]{0:T(128)S(6)} %sub.72.which_ref, bf16[108,2,16,256]{3,2,1,0:T(8,128)(2,1)} %own_ref.3), custom_call_target="tpu_custom_call" | custom-call | tf_op jit(solution)/shard_map/take_rows/pallas_call | solution.py:159
  10.9 1.6 %collective-permute-start.18 = (bf16[108,2,8,256]{3,2,1,0:T(8,128)(2,1)}, bf16[108,2,8,256]{3,2,1,0:T(8,128)(2,1)S(1)}, u32[]{:S(2)}, u32[]{:S(2)}) collective-permute-start(bf16[108,2,8,256]{3,2,1,0:T(8,128)(2,1)} %take_rows.1), channel_id=1, source_target_pairs={{0,16},{16,0},{1,17},{17,1},{2,18},{18,2},{3,19},{19,3},{4,20},{20... | collective-permute-start | bytes 2654216 | tf_op jit(solution)/shard_map/ppermute | solution.py:487
  13.6 1.5 %collective-permute-done.5.refs_6_ = bf16[112,640]{1,0:T(8,128)(2,1)S(1)} collective-permute-done((bf16[112,640]{1,0:T(8,128)(2,1)S(1)}, bf16[112,640]{1,0:T(8,128)(2,1)S(1)}, u32[]{:S(2)}, u32[]{:S(2)}) %collective-permute-start.5) | collective-permute-done | bytes 143392 | tf_op jit(solution)/shard_map/ppermute | solution.py:420
  15.3 1.6 %collective-permute-start.6 = (bf16[112,640]{1,0:T(8,128)(2,1)S(1)}, bf16[112,640]{1,0:T(8,128)(2,1)S(1)}, u32[]{:S(2)}, u32[]{:S(2)}) collective-permute-start(bf16[112,640]{1,0:T(8,128)(2,1)S(1)} %collective-permute-done.5.refs_6_), channel_id=1, source_target_pairs={{0,1},{1,0},{2,3},{3,2},{4,5},{5,4},{6,7},{7,6},{8,9},{9,8},{10,11... | collective-permute-start | bytes 430088 | tf_op jit(solution)/shard_map/ppermute | solution.py:420
  18.2 1.5 %collective-permute-start.2 = (bf16[112,640]{1,0:T(8,128)(2,1)S(1)}, bf16[112,640]{1,0:T(8,128)(2,1)S(1)}, u32[]{:S(2)}, u32[]{:S(2)}) collective-permute-start(bf16[112,640]{1,0:T(8,128)(2,1)S(1)} %collective-permute-done.1.refs_2_), channel_id=1, source_target_pairs={{0,1},{1,0},{2,3},{3,2},{4,5},{5,4},{6,7},{7,6},{8,9},{9,8},{10,11... | collective-permute-start | bytes 430088 | tf_op jit(solution)/shard_map/ppermute | solution.py:420
  19.7 3.3 %collective-permute-done.13.refs_14_ = bf16[112,640]{1,0:T(8,128)(2,1)S(1)} collective-permute-done((bf16[112,640]{1,0:T(8,128)(2,1)S(1)}, bf16[112,640]{1,0:T(8,128)(2,1)S(1)}, u32[]{:S(2)}, u32[]{:S(2)}) %collective-permute-start.13) | collective-permute-done | bytes 143392 | tf_op jit(solution)/shard_map/ppermute | solution.py:420
  23.7 1.4 %collective-permute-done.11.refs_12_ = bf16[112,640]{1,0:T(8,128)(2,1)S(1)} collective-permute-done((bf16[112,640]{1,0:T(8,128)(2,1)S(1)}, bf16[112,640]{1,0:T(8,128)(2,1)S(1)}, u32[]{:S(2)}, u32[]{:S(2)}) %collective-permute-start.11) | collective-permute-done | bytes 143392 | tf_op jit(solution)/shard_map/ppermute | solution.py:420
  25.6 5.2 %collective-permute-done.7.refs_8_ = bf16[112,640]{1,0:T(8,128)(2,1)S(1)} collective-permute-done((bf16[112,640]{1,0:T(8,128)(2,1)S(1)}, bf16[112,640]{1,0:T(8,128)(2,1)S(1)}, u32[]{:S(2)}, u32[]{:S(2)}) %collective-permute-start.7) | collective-permute-done | bytes 143392 | tf_op jit(solution)/shard_map/ppermute | solution.py:420
  33.8 9.3 %density_part.5 = (bf16[36,2,8,256]{3,2,1,0:T(8,128)(2,1)}, bf16[36,2,8,128]{3,2,1,0:T(8,128)(2,1)}, bf16[36,2,8,128]{3,2,1,0:T(8,128)(2,1)}) custom-call(s32[36]{0:T(128)} %get-tuple-element.46.order_ref, s32[36]{0:T(128)} %get-tuple-element.43.tiles_ref, bf16[256,256]{1,0:T(8,128)(2,1)} %and_convert_fusion.spread_ref, bf16[112,640]{1,0:T(8,128)(2,1)} %copy-done.1, ...), custom_call_target="tpu_custom_call" | custom-call | tf_op jit(solution)/shard_map/density_part/pallas_call | solution.py:115
  43.1 1.1 %collective-permute-start.21 = (bf16[36,2,8,128]{3,2,1,0:T(8,128)(2,1)}, bf16[36,2,8,128]{3,2,1,0:T(8,128)(2,1)S(1)}, u32[]{:S(2)}, u32[]{:S(2)}) collective-permute-start(bf16[36,2,8,128]{3,2,1,0:T(8,128)(2,1)} %get-tuple-element.32), channel_id=1, source_target_pairs={{0,16},{16,0},{1,17},{17,1},{2,18},{18,2},{3,19},{19,3},{4,20},{20... | collective-permute-start | bytes 442376 | tf_op jit(solution)/shard_map/ppermute | solution.py:505
  44.2 9.3 %density_part.4 = (bf16[36,2,8,256]{3,2,1,0:T(8,128)(2,1)}, bf16[36,2,8,128]{3,2,1,0:T(8,128)(2,1)}, bf16[36,2,8,128]{3,2,1,0:T(8,128)(2,1)}) custom-call(s32[36]{0:T(128)} %get-tuple-element.47.order_ref, s32[36]{0:T(128)} %get-tuple-element.44.tiles_ref, bf16[256,256]{1,0:T(8,128)(2,1)} %and_convert_fusion.spread_ref, bf16[112,640]{1,0:T(8,128)(2,1)} %copy-done.1, ...), custom_call_target="tpu_custom_call" | custom-call | tf_op jit(solution)/shard_map/density_part/pallas_call | solution.py:115
  54.6 8.9 %density_part.3 = (bf16[36,2,8,256]{3,2,1,0:T(8,128)(2,1)}, bf16[36,2,8,128]{3,2,1,0:T(8,128)(2,1)}, bf16[36,2,8,128]{3,2,1,0:T(8,128)(2,1)}) custom-call(s32[36]{0:T(128)} %get-tuple-element.48.order_ref, s32[36]{0:T(128)} %get-tuple-element.45.tiles_ref, bf16[256,256]{1,0:T(8,128)(2,1)} %and_convert_fusion.spread_ref, bf16[112,640]{1,0:T(8,128)(2,1)} %copy-done.1, ...), custom_call_target="tpu_custom_call" | custom-call | tf_op jit(solution)/shard_map/density_part/pallas_call | solution.py:115
  63.6 1.4 %collective-permute-start.19 = (bf16[36,2,8,128]{3,2,1,0:T(8,128)(2,1)}, bf16[36,2,8,128]{3,2,1,0:T(8,128)(2,1)S(1)}, u32[]{:S(2)}, u32[]{:S(2)}) collective-permute-start(bf16[36,2,8,128]{3,2,1,0:T(8,128)(2,1)} %get-tuple-element.30), channel_id=1, source_target_pairs={{0,16},{16,0},{1,17},{17,1},{2,18},{18,2},{3,19},{19,3},{4,20},{20... | collective-permute-start | bytes 442376 | tf_op jit(solution)/shard_map/ppermute | solution.py:505
  65.7 1.4 %collective-permute-start.16 = (bf16[36,2,8,128]{3,2,1,0:T(8,128)(2,1)S(1)}, bf16[36,2,8,128]{3,2,1,0:T(8,128)(2,1)S(1)}, u32[]{:S(2)}, u32[]{:S(2)}) collective-permute-start(bf16[36,2,8,128]{3,2,1,0:T(8,128)(2,1)S(1)} %copy-done.25), channel_id=1, source_target_pairs={{0,16},{16,0},{1,17},{17,1},{2,18},{18,2},{3,19},{19,3},{4,20},{20... | collective-permute-start | bytes 442376 | tf_op jit(solution)/shard_map/ppermute | solution.py:505
  68.0 3.3 %coulomb_transform.3.refs_6_ = f32[2,6,3,6,2,8,128]{6,5,4,3,2,1,0:T(8,128)} custom-call(s32[1]{0:T(128)} %bitcast.which_ref, bf16[108,2,16,256]{3,2,1,0:T(8,128)(2,1)} %own_ref.3, bf16[108,2,8,256]{3,2,1,0:T(8,128)(2,1)} %copy-done), custom_call_target="tpu_custom_call" | custom-call | tf_op jit(solution)/shard_map/coulomb_transform/pallas_call | solution.py:257
  72.0 4.5 %convolve.2 = (bf16[108,2,16,256]{3,2,1,0:T(8,128)(2,1)}, bf16[108,2,8,128]{3,2,1,0:T(8,128)(2,1)}) custom-call(s32[1]{0:T(128)} %bitcast.which_ref, bf16[36,2,8,256]{3,2,1,0:T(8,128)(2,1)} %get-tuple-element.24.refs_0_, bf16[36,2,8,256]{3,2,1,0:T(8,128)(2,1)} %get-tuple-element.25.refs_1_, bf16[36,2,8,256]{3,2,1,0:T(8,128)(2,1)} %get-tuple-element.26.refs_2_, ...), custom_call_target="tpu_custom_call" | custom-call | tf_op jit(solution)/shard_map/convolve/pallas_call | solution.py:328
  77.7 3.3 %coulomb_transform.2.refs_6_ = f32[2,6,3,6,2,8,128]{6,5,4,3,2,1,0:T(8,128)} custom-call(s32[1]{0:T(128)} %bitcast.which_ref, bf16[108,2,16,256]{3,2,1,0:T(8,128)(2,1)} %own_ref.3, bf16[108,2,8,256]{3,2,1,0:T(8,128)(2,1)} %copy-done), custom_call_target="tpu_custom_call" | custom-call | tf_op jit(solution)/shard_map/coulomb_transform/pallas_call | solution.py:257
  81.7 4.5 %convolve.3 = (bf16[108,2,16,256]{3,2,1,0:T(8,128)(2,1)}, bf16[108,2,8,128]{3,2,1,0:T(8,128)(2,1)}) custom-call(s32[1]{0:T(128)} %bitcast.which_ref, bf16[36,2,8,256]{3,2,1,0:T(8,128)(2,1)} %get-tuple-element.24.refs_0_, bf16[36,2,8,256]{3,2,1,0:T(8,128)(2,1)} %get-tuple-element.25.refs_1_, ...), custom_call_target="tpu_custom_call", output_to_operand_aliasing={{0}: (8, {})} | custom-call | tf_op jit(solution)/shard_map/convolve/pallas_call | solution.py:328
  87.2 1.8 %collective-permute-done.22 = bf16[108,2,8,128]{3,2,1,0:T(8,128)(2,1)S(1)} collective-permute-done((bf16[108,2,8,128]{3,2,1,0:T(8,128)(2,1)}, bf16[108,2,8,128]{3,2,1,0:T(8,128)(2,1)S(1)}, u32[]{:S(2)}, u32[]{:S(2)}) %collective-permute-start.22) | collective-permute-done | bytes 442400 | tf_op jit(solution)/shard_map/ppermute | solution.py:511
  89.8 7.8 %collective-permute-done.23 = bf16[108,2,8,128]{3,2,1,0:T(8,128)(2,1)S(1)} collective-permute-done((bf16[108,2,8,128]{3,2,1,0:T(8,128)(2,1)}, bf16[108,2,8,128]{3,2,1,0:T(8,128)(2,1)S(1)}, u32[]{:S(2)}, u32[]{:S(2)}) %collective-permute-start.23) | collective-permute-done | bytes 442400 | tf_op jit(solution)/shard_map/ppermute | solution.py:511
  (107 shorter events, 15.6 us)
Async XLA Ops:
  2.7 12.6 %collective-permute-start.9 = (bf16[112,640]{1,0:T(8,128)(2,1)S(1)}, bf16[112,640]{1,0:T(8,128)(2,1)S(1)}, u32[]{:S(2)}, u32[]{:S(2)}) collective-permute-start(bf16[112,640]{1,0:T(8,128)(2,1)S(1)} %fusion.7.refs_0_), channel_id=1, source_target_pairs={{0,2},{1,3},{2,0},{3,1},{4,6},{5,7},{6,4},{7,5},{8,10},{9,11},{10,... | collective-permute-start | bytes 430088 | tf_op jit(solution)/shard_map/ppermute | solution.py:420
  5.8 9.3 %collective-permute-start.5 = (bf16[112,640]{1,0:T(8,128)(2,1)S(1)}, bf16[112,640]{1,0:T(8,128)(2,1)S(1)}, u32[]{:S(2)}, u32[]{:S(2)}) collective-permute-start(bf16[112,640]{1,0:T(8,128)(2,1)S(1)} %fusion.7.refs_0_), channel_id=1, source_target_pairs={{0,6},{1,15},{2,4},{3,13},{4,10},{5,3},{6,8},{7,1},{8,14},{9,7},{1... | collective-permute-start | bytes 430088 | tf_op jit(solution)/shard_map/ppermute | solution.py:420
  7.3 9.6 %collective-permute-start.1 = (bf16[112,640]{1,0:T(8,128)(2,1)S(1)}, bf16[112,640]{1,0:T(8,128)(2,1)S(1)}, u32[]{:S(2)}, u32[]{:S(2)}) collective-permute-start(bf16[112,640]{1,0:T(8,128)(2,1)S(1)} %fusion.7.refs_0_), channel_id=1, source_target_pairs={{0,4},{1,13},{2,6},{3,15},{4,8},{5,1},{6,10},{7,3},{8,12},{9,5},{1... | collective-permute-start | bytes 430088 | tf_op jit(solution)/shard_map/ppermute | solution.py:420
  8.9 8.4 %collective-permute-start = (bf16[112,640]{1,0:T(8,128)(2,1)S(1)}, bf16[112,640]{1,0:T(8,128)(2,1)S(1)}, u32[]{:S(2)}, u32[]{:S(2)}) collective-permute-start(bf16[112,640]{1,0:T(8,128)(2,1)S(1)} %fusion.7.refs_0_), channel_id=1, source_target_pairs={{0,1},{1,0},{2,3},{3,2},{4,5},{5,4},{6,7},{7,6},{8,9},{9,8},{10,11... | collective-permute-start | bytes 430088 | tf_op jit(solution)/shard_map/ppermute | solution.py:420
  10.9 56.2 %collective-permute-start.18 = (bf16[108,2,8,256]{3,2,1,0:T(8,128)(2,1)}, bf16[108,2,8,256]{3,2,1,0:T(8,128)(2,1)S(1)}, u32[]{:S(2)}, u32[]{:S(2)}) collective-permute-start(bf16[108,2,8,256]{3,2,1,0:T(8,128)(2,1)} %take_rows.1), channel_id=1, source_target_pairs={{0,16},{16,0},{1,17},{17,1},{2,18},{18,2},{3,19},{19,3},{4,20},{20... | collective-permute-start | bytes 2654216 | tf_op jit(solution)/shard_map/ppermute | solution.py:487
  15.1 7.9 %collective-permute-start.13 = (bf16[112,640]{1,0:T(8,128)(2,1)S(1)}, bf16[112,640]{1,0:T(8,128)(2,1)S(1)}, u32[]{:S(2)}, u32[]{:S(2)}) collective-permute-start(bf16[112,640]{1,0:T(8,128)(2,1)S(1)} %collective-permute-done.5.refs_6_), channel_id=1, source_target_pairs={{0,4},{1,13},{2,6},{3,15},{4,8},{5,1},{6,10},{7,3},{8,12},{9,5},{1... | collective-permute-start | bytes 430088 | tf_op jit(solution)/shard_map/ppermute | solution.py:420
  15.3 7.8 %collective-permute-start.6 = (bf16[112,640]{1,0:T(8,128)(2,1)S(1)}, bf16[112,640]{1,0:T(8,128)(2,1)S(1)}, u32[]{:S(2)}, u32[]{:S(2)}) collective-permute-start(bf16[112,640]{1,0:T(8,128)(2,1)S(1)} %collective-permute-done.5.refs_6_), channel_id=1, source_target_pairs={{0,1},{1,0},{2,3},{3,2},{4,5},{5,4},{6,7},{7,6},{8,9},{9,8},{10,11... | collective-permute-start | bytes 430088 | tf_op jit(solution)/shard_map/ppermute | solution.py:420
  16.9 1.4 %collective-permute-start.10 = (bf16[112,640]{1,0:T(8,128)(2,1)S(1)}, bf16[112,640]{1,0:T(8,128)(2,1)S(1)}, u32[]{:S(2)}, u32[]{:S(2)}) collective-permute-start(bf16[112,640]{1,0:T(8,128)(2,1)S(1)} %collective-permute-done.9.refs_10_), channel_id=1, source_target_pairs={{0,1},{1,0},{2,3},{3,2},{4,5},{5,4},{6,7},{7,6},{8,9},{9,8},{10,11... | collective-permute-start | bytes 430088 | tf_op jit(solution)/shard_map/ppermute | solution.py:420
  17.3 7.8 %collective-permute-start.11 = (bf16[112,640]{1,0:T(8,128)(2,1)S(1)}, bf16[112,640]{1,0:T(8,128)(2,1)S(1)}, u32[]{:S(2)}, u32[]{:S(2)}) collective-permute-start(bf16[112,640]{1,0:T(8,128)(2,1)S(1)} %collective-permute-done.1.refs_2_), channel_id=1, source_target_pairs={{0,4},{1,13},{2,6},{3,15},{4,8},{5,1},{6,10},{7,3},{8,12},{9,5},{1... | collective-permute-start | bytes 430088 | tf_op jit(solution)/shard_map/ppermute | solution.py:420
  18.2 6.9 %collective-permute-start.2 = (bf16[112,640]{1,0:T(8,128)(2,1)S(1)}, bf16[112,640]{1,0:T(8,128)(2,1)S(1)}, u32[]{:S(2)}, u32[]{:S(2)}) collective-permute-start(bf16[112,640]{1,0:T(8,128)(2,1)S(1)} %collective-permute-done.1.refs_2_), channel_id=1, source_target_pairs={{0,1},{1,0},{2,3},{3,2},{4,5},{5,4},{6,7},{7,6},{8,9},{9,8},{10,11... | collective-permute-start | bytes 430088 | tf_op jit(solution)/shard_map/ppermute | solution.py:420
  23.1 7.8 %collective-permute-start.7 = (bf16[112,640]{1,0:T(8,128)(2,1)S(1)}, bf16[112,640]{1,0:T(8,128)(2,1)S(1)}, u32[]{:S(2)}, u32[]{:S(2)}) collective-permute-start(bf16[112,640]{1,0:T(8,128)(2,1)S(1)} %collective-permute-done.refs_1_), channel_id=1, source_target_pairs={{0,6},{1,15},{2,4},{3,13},{4,10},{5,3},{6,8},{7,1},{8,14},{9,7},{1... | collective-permute-start | bytes 430088 | tf_op jit(solution)/shard_map/ppermute | solution.py:420
  23.1 8.7 %collective-permute-start.3 = (bf16[112,640]{1,0:T(8,128)(2,1)S(1)}, bf16[112,640]{1,0:T(8,128)(2,1)S(1)}, u32[]{:S(2)}, u32[]{:S(2)}) collective-permute-start(bf16[112,640]{1,0:T(8,128)(2,1)S(1)} %collective-permute-done.refs_1_), channel_id=1, source_target_pairs={{0,4},{1,13},{2,6},{3,15},{4,8},{5,1},{6,10},{7,3},{8,12},{9,5},{1... | collective-permute-start | bytes 430088 | tf_op jit(solution)/shard_map/ppermute | solution.py:420
  25.1 7.3 %collective-permute-start.14 = (bf16[112,640]{1,0:T(8,128)(2,1)S(1)}, bf16[112,640]{1,0:T(8,128)(2,1)S(1)}, u32[]{:S(2)}, u32[]{:S(2)}) collective-permute-start(bf16[112,640]{1,0:T(8,128)(2,1)S(1)} %collective-permute-done.13.refs_14_), channel_id=1, source_target_pairs={{0,1},{1,0},{2,3},{3,2},{4,5},{5,4},{6,7},{7,6},{8,9},{9,8},{10,11... | collective-permute-start | bytes 430088 | tf_op jit(solution)/shard_map/ppermute | solution.py:420
  25.1 7.3 %collective-permute-start.12 = (bf16[112,640]{1,0:T(8,128)(2,1)S(1)}, bf16[112,640]{1,0:T(8,128)(2,1)S(1)}, u32[]{:S(2)}, u32[]{:S(2)}) collective-permute-start(bf16[112,640]{1,0:T(8,128)(2,1)S(1)} %collective-permute-done.11.refs_12_), channel_id=1, source_target_pairs={{0,1},{1,0},{2,3},{3,2},{4,5},{5,4},{6,7},{7,6},{8,9},{9,8},{10,11... | collective-permute-start | bytes 430088 | tf_op jit(solution)/shard_map/ppermute | solution.py:420
  30.9 1.6 %collective-permute-start.8 = (bf16[112,640]{1,0:T(8,128)(2,1)S(1)}, bf16[112,640]{1,0:T(8,128)(2,1)S(1)}, u32[]{:S(2)}, u32[]{:S(2)}) collective-permute-start(bf16[112,640]{1,0:T(8,128)(2,1)S(1)} %collective-permute-done.7.refs_8_), channel_id=1, source_target_pairs={{0,1},{1,0},{2,3},{3,2},{4,5},{5,4},{6,7},{7,6},{8,9},{9,8},{10,11... | collective-permute-start | bytes 430088 | tf_op jit(solution)/shard_map/ppermute | solution.py:420
  31.8 1.4 %collective-permute-start.4 = (bf16[112,640]{1,0:T(8,128)(2,1)S(1)}, bf16[112,640]{1,0:T(8,128)(2,1)S(1)}, u32[]{:S(2)}, u32[]{:S(2)}) collective-permute-start(bf16[112,640]{1,0:T(8,128)(2,1)S(1)} %collective-permute-done.3.refs_4_), channel_id=1, source_target_pairs={{0,1},{1,0},{2,3},{3,2},{4,5},{5,4},{6,7},{7,6},{8,9},{9,8},{10,11... | collective-permute-start | bytes 430088 | tf_op jit(solution)/shard_map/ppermute | solution.py:420
  43.1 22.5 %collective-permute-start.21 = (bf16[36,2,8,128]{3,2,1,0:T(8,128)(2,1)}, bf16[36,2,8,128]{3,2,1,0:T(8,128)(2,1)S(1)}, u32[]{:S(2)}, u32[]{:S(2)}) collective-permute-start(bf16[36,2,8,128]{3,2,1,0:T(8,128)(2,1)} %get-tuple-element.32), channel_id=1, source_target_pairs={{0,16},{16,0},{1,17},{17,1},{2,18},{18,2},{3,19},{19,3},{4,20},{20... | collective-permute-start | bytes 442376 | tf_op jit(solution)/shard_map/ppermute | solution.py:505
  53.5 17.8 %collective-permute-start.20 = (bf16[36,2,8,128]{3,2,1,0:T(8,128)(2,1)}, bf16[36,2,8,128]{3,2,1,0:T(8,128)(2,1)S(1)}, u32[]{:S(2)}, u32[]{:S(2)}) collective-permute-start(bf16[36,2,8,128]{3,2,1,0:T(8,128)(2,1)} %get-tuple-element.31), channel_id=1, source_target_pairs={{0,16},{16,0},{1,17},{17,1},{2,18},{18,2},{3,19},{19,3},{4,20},{20... | collective-permute-start | bytes 442376 | tf_op jit(solution)/shard_map/ppermute | solution.py:505
  63.6 7.8 %collective-permute-start.19 = (bf16[36,2,8,128]{3,2,1,0:T(8,128)(2,1)}, bf16[36,2,8,128]{3,2,1,0:T(8,128)(2,1)S(1)}, u32[]{:S(2)}, u32[]{:S(2)}) collective-permute-start(bf16[36,2,8,128]{3,2,1,0:T(8,128)(2,1)} %get-tuple-element.30), channel_id=1, source_target_pairs={{0,16},{16,0},{1,17},{17,1},{2,18},{18,2},{3,19},{19,3},{4,20},{20... | collective-permute-start | bytes 442376 | tf_op jit(solution)/shard_map/ppermute | solution.py:505
  65.0 16.0 %collective-permute-start.17 = (bf16[36,2,8,128]{3,2,1,0:T(8,128)(2,1)S(1)}, bf16[36,2,8,128]{3,2,1,0:T(8,128)(2,1)S(1)}, u32[]{:S(2)}, u32[]{:S(2)}) collective-permute-start(bf16[36,2,8,128]{3,2,1,0:T(8,128)(2,1)S(1)} %copy-done.24), channel_id=1, source_target_pairs={{0,16},{16,0},{1,17},{17,1},{2,18},{18,2},{3,19},{19,3},{4,20},{20... | collective-permute-start | bytes 442376 | tf_op jit(solution)/shard_map/ppermute | solution.py:505
  65.7 15.3 %collective-permute-start.16 = (bf16[36,2,8,128]{3,2,1,0:T(8,128)(2,1)S(1)}, bf16[36,2,8,128]{3,2,1,0:T(8,128)(2,1)S(1)}, u32[]{:S(2)}, u32[]{:S(2)}) collective-permute-start(bf16[36,2,8,128]{3,2,1,0:T(8,128)(2,1)S(1)} %copy-done.25), channel_id=1, source_target_pairs={{0,16},{16,0},{1,17},{17,1},{2,18},{18,2},{3,19},{19,3},{4,20},{20... | collective-permute-start | bytes 442376 | tf_op jit(solution)/shard_map/ppermute | solution.py:505
  67.1 13.9 %collective-permute-start.15 = (bf16[36,2,8,128]{3,2,1,0:T(8,128)(2,1)}, bf16[36,2,8,128]{3,2,1,0:T(8,128)(2,1)S(1)}, u32[]{:S(2)}, u32[]{:S(2)}) collective-permute-start(bf16[36,2,8,128]{3,2,1,0:T(8,128)(2,1)} %get-tuple-element.27), channel_id=1, source_target_pairs={{0,16},{16,0},{1,17},{17,1},{2,18},{18,2},{3,19},{19,3},{4,20},{20... | collective-permute-start | bytes 442376 | tf_op jit(solution)/shard_map/ppermute | solution.py:505
  76.6 12.4 %collective-permute-start.22 = (bf16[108,2,8,128]{3,2,1,0:T(8,128)(2,1)}, bf16[108,2,8,128]{3,2,1,0:T(8,128)(2,1)S(1)}, u32[]{:S(2)}, u32[]{:S(2)}) collective-permute-start(bf16[108,2,8,128]{3,2,1,0:T(8,128)(2,1)} %get-tuple-element.35), channel_id=1, source_target_pairs={{0,16},{16,0},{1,17},{17,1},{2,18},{18,2},{3,19},{19,3},{4,20},{20... | collective-permute-start | bytes 1327112 | tf_op jit(solution)/shard_map/ppermute | solution.py:511
  86.3 11.3 %collective-permute-start.23 = (bf16[108,2,8,128]{3,2,1,0:T(8,128)(2,1)}, bf16[108,2,8,128]{3,2,1,0:T(8,128)(2,1)S(1)}, u32[]{:S(2)}, u32[]{:S(2)}) collective-permute-start(bf16[108,2,8,128]{3,2,1,0:T(8,128)(2,1)} %get-tuple-element.36), channel_id=1, source_target_pairs={{0,16},{16,0},{1,17},{17,1},{2,18},{18,2},{3,19},{19,3},{4,20},{20... | collective-permute-start | bytes 1327112 | tf_op jit(solution)/shard_map/ppermute | solution.py:511
  (26 other events, 198.5 us)
where the time goes:
time: 98.9 us; the launch traced here: 98.4 us
  Pallas kernels  45.2 us (46%)
  waiting for transfers between devices  23.5 us (24%)
  starting transfers between devices  20.1 us (20%)
  local copies, waits for them, and re-layouts  6.96 us (7%)
  other arithmetic  2.28 us (2%)
    pallas_call x3, Pallas kernels, density_part(): pl.pallas_call(kernel, out_shape=(kept,) + (sent,) * splits, in_specs=[sc...  27.5 us
    ppermute x15, waiting for transfers between devices, move(): return lax.ppermute(value, 'pts', pairs)  13.9 us
    ppermute x15, starting transfers between devices, move(): return lax.ppermute(value, 'pts', pairs)  10.1 us
    ppermute x2, waiting for transfers between devices, local_pair(): returned.append(lax.ppermute(sent, 'ka', swap))  9.62 us
    pallas_call x2, Pallas kernels, convolve(): pl.pallas_call(kernel, out_shape=(jax.ShapeDtypeStruct((count, 2, 2 * row...  9.08 us
    pallas_call x2, Pallas kernels, coulomb_transform(): pl.pallas_call(kernel, out_shape=jax.ShapeDtypeStruct(shape, jnp.float32)...  6.58 us
    ppermute x6, starting transfers between devices, local_pair(): other[i].append(lax.ppermute(value, 'ka', swap))  6.39 us
    unnamed x52, local copies, waits for them, and re-layouts  2.3 us
  transfers between devices with their start and end apart: 24, of which 9 were waited for; matrix products, arithmetic and copies ran while one was open for 4% of the time, Pallas kernels for 46%

commit v1 on v0

--- a/solution.py
+++ b/solution.py
@@ -16,20 +16,22 @@
 LANE_HALF = LANES // 2
 GROUP = 6
 AHEAD = 2
+PARTS = ((0, 2), (2, 1))
 BLOCK = 16
 
 
-def band_order(counts, parts):
-    tiles = -(-counts.reshape(parts, -1) // LANES)
-    size = tiles.shape[1]
-    index = jnp.arange(size, dtype=jnp.int32)
-    key = tiles * size - index
-    rank = jnp.sum((key[:, None, :] > key[:, :, None]).astype(jnp.int32), 2)
-    hit = (rank[:, :, None] == index).astype(jnp.int32)
-    return jnp.sum(hit * index[:, None], 1), jnp.sum(hit * tiles[:, :, None], 1)
-
-
-def density_part(spread, order, tiles, parts, orbitals, start, count):
+def band_order(counts, size):
+    tiles = -(-counts // LANES)
+    index = jnp.arange(counts.shape[0], dtype=jnp.int32)
+    part = jnp.where(index < PARTS[1][0] * size, 0, PARTS[1][0] * size)
+    key = tiles * counts.shape[0] - index
+    same = part[:, None] == part[None, :]
+    rank = part + jnp.sum((same & (key[None, :] > key[:, None])).astype(jnp.int32), 1)
+    hit = (rank[:, None] == index[None, :]).astype(jnp.int32)
+    return jnp.sum(hit * (index - part)[:, None], 0), jnp.sum(hit * tiles[:, None], 0)
+
+
+def density_part(spread, order, tiles, parts, orbitals, start, count, splits):
     rows = len(parts)
     width = parts[0].shape[1]
     columns, slots = orbitals.shape[2:]
@@ -42,7 +44,7 @@
     ring = ahead + 1
     whole = (slots // LANES - 1) * LANES
     depth = slots // LANES
-    splits = columns // LANES
+    chunk = columns // splits
 
     def kernel(order_ref, tiles_ref, spread_ref, *refs):
         sources, orb, refs = refs[:rows], refs[rows], refs[rows + 1 :]
@@ -53,13 +55,13 @@
 
         def per_class(g, act):
             for n in range(1, depth + 1):
-                pl.when(tiles_ref[g * group] == n)(lambda n=n: act(n))
+                pl.when(tiles_ref[start + g * group] == n)(lambda n=n: act(n))
 
         def panels(g, n, act):
             lanes = pl.ds(0, n * LANES)
             for u in range(group):
                 slot = g % ring * group + u
-                source = orb.at[start + order_ref[g * group + u], :, :, lanes]
+                source = orb.at[start + order_ref[start + g * group + u], :, :, lanes]
                 act(pltpu.make_async_copy(source, buf.at[slot, :, :, lanes], sem.at[slot]))
 
         for copy in row_copies:
@@ -83,7 +85,7 @@
         def gram(g, n):
             panels(g, n, lambda copy: copy.wait())
             for u in range(group):
-                k = order_ref[g * group + u]
+                k = order_ref[start + g * group + u]
                 slot = g % ring * group + u
                 row = pl.ds(pl.multiple_of((k + skip) * rows, rows), rows)
                 re = left[row, : n * LANES]
@@ -94,8 +96,8 @@
                 keep_ref[k, 0] = out[:keep]
                 keep_ref[k, 1] = out[rows : rows + keep]
                 for j in range(splits):
-                    send_refs[j][k, 0] = out[keep:rows, j * LANES : (j + 1) * LANES]
-                    send_refs[j][k, 1] = out[rows + keep :, j * LANES : (j + 1) * LANES]
+                    send_refs[j][k, 0] = out[keep:rows, j * chunk : (j + 1) * chunk]
+                    send_refs[j][k, 1] = out[rows + keep :, j * chunk : (j + 1) * chunk]
 
         def step(g, _):
             @pl.when(g + ahead < groups)
@@ -111,7 +113,7 @@
     local = pl.BlockSpec(memory_space=pltpu.VMEM)
     scalars = pl.BlockSpec(memory_space=pltpu.SMEM)
     kept = jax.ShapeDtypeStruct((count, 2, keep, columns), jnp.bfloat16)
-    sent = jax.ShapeDtypeStruct((count, 2, keep, LANES), jnp.bfloat16)
+    sent = jax.ShapeDtypeStruct((count, 2, keep, chunk), jnp.bfloat16)
     return pl.pallas_call(
         kernel,
         out_shape=(kept,) + (sent,) * splits,
@@ -207,9 +209,10 @@
     for kx in range(HALF):
 
         def body(ky, _):
-            base = ky * KSIDE + kx * KSIDE * KSIDE * (1 if len(own) == 1 else 0)
-            mine = [load(own[kx % len(own)], base + kz) for kz in range(KSIDE)]
-            theirs = [load(other[kx % len(other)], base + kz) for kz in range(KSIDE)]
+            part = max(i for i in range(len(own)) if PARTS[i][0] <= kx)
+            base = ky * KSIDE + (kx - PARTS[part][0]) * KSIDE * KSIDE
+            mine = [load(own[part], base + kz) for kz in range(KSIDE)]
+            theirs = [load(other[part], base + kz) for kz in range(KSIDE)]
             plus = six([add(a, b) for a, b in zip(mine, theirs)])
             minus = six([sub(b, a) if kx % 2 else sub(a, b) for a, b in zip(mine, theirs)])
             for sign, values in enumerate((plus, minus)):
@@ -321,9 +324,12 @@
 
     shape = (2, KSIDE, HALF, KSIDE, 2, rows, LANES)
     block = (count, 2, rows, LANES)
-    plane = pl.BlockSpec((count // planes, 2, rows, LANES), lambda i, w: (0, 0, 0, column))
-    come = pl.BlockSpec((count // planes, 2, rows, LANES), lambda i, w: (0, 0, 0, 0))
-    specs = [plane] * planes + [come] * planes + [pl.BlockSpec(shape, lambda i, w: (0,) * 7)]
+
+    def plane(value):
+        at = column if value.shape[3] == columns else 0
+        return pl.BlockSpec(value.shape[:3] + (LANES,), lambda i, w: (0, 0, 0, at))
+
+    specs = [plane(value) for value in (*own, *other)] + [pl.BlockSpec(shape, lambda i, w: (0,) * 7)]
     extra = () if whole is None else (whole,)
     return pl.pallas_call(
         kernel,
@@ -478,7 +484,7 @@
 
 def local_pair(orbitals, counts, occupation, coulomb):
     swap = [(0, 1), (1, 0)]
-    count, _, columns, _ = orbitals.shape
+    _, _, columns, _ = orbitals.shape
     rows = coulomb.shape[2]
     keep = rows // 2
     half = lax.axis_index("ka")
@@ -493,16 +499,18 @@
     spread = (place[:, None] // rows == place[None, :] % BLOCK) & (place[:, None] % rows == target[None, :])
     spread = spread.astype(jnp.bfloat16)
     splits = columns // LANES
-    order, tiles = band_order(counts, HALF)
+    size = KSIDE * KSIDE
+    order, tiles = band_order(counts, size)
     order, tiles, spread = lax.optimization_barrier((order, tiles, spread))
-    size = count // HALF
     own, other = [], []
-    for i in range(HALF):
-        kept, *sent = density_part(spread, order[i], tiles[i], parts, orbitals, i * size, size)
+    for i, (plane, planes) in enumerate(PARTS):
+        cuts = 1 if i + 1 < len(PARTS) else splits
+        kept, *sent = density_part(spread, order, tiles, parts, orbitals, plane * size, planes * size, cuts)
         own.append(kept)
         other.append([])
         for value in sent:
             other[i].append(lax.ppermute(value, "ka", swap))
+    other[:-1] = [value * splits for value in other[:-1]]
     whole = None
     returned = []
     for j in range(splits):

time: 98.9 us -> 94.6 us (0.957)
  Pallas kernels: 45.2 us -> 40.9 us
  waiting for transfers between devices: 23.5 us -> 25.3 us
  starting transfers between devices: 20.1 us -> 18.4 us
    pallas_call x3 -> x2, Pallas kernels: 27.5 us -> 23.3 us  [density_part(): pl.pallas_call(kernel, out_shape=(kept,) + (sent,) * splits, in_specs=[sc...]
    ppermute x6 -> x3, starting transfers between devices: 6.39 us -> 3.65 us  [local_pair(): other[i].append(lax.ppermute(value, 'ka', swap))]
    ppermute x6 -> x3, waiting for transfers between devices: 0.02 us -> 2.46 us  [local_pair(): other[i].append(lax.ppermute(value, 'ka', swap))]
    squeeze x2 -> x0, local copies, waits for them, and re-layouts: 1.22 us -> none  [the longest x1 0.63 us: local_pair(): tiles[i]]
    ppermute x15, starting transfers between devices: 10.1 us -> 11.1 us  [move(): return lax.ppermute(value, 'pts', pairs)]
    unnamed x52 -> x42, local copies, waits for them, and re-layouts: 2.3 us -> 3.18 us
  transfers between devices with their start and end apart: 24 -> 21, of which waited for: 9 -> 9; matrix products, arithmetic and copies ran while one was open for 4% -> 3% of each run, Pallas kernels for 46% -> 43%
where the time goes in v1:
time: 94.6 us; the launch traced here: 94.2 us
  Pallas kernels  40.9 us (43%)
  waiting for transfers between devices  25.3 us (27%)
  starting transfers between devices  18.4 us (19%)
  local copies, waits for them, and re-layouts  6.55 us (7%)
  other arithmetic  2.84 us (3%)
    pallas_call x2, Pallas kernels, density_part(): pl.pallas_call(kernel, out_shape=(kept,) + (sent,) * splits, in_specs=[sc...  23.3 us
    ppermute x15, waiting for transfers between devices, move(): return lax.ppermute(value, 'pts', pairs)  12.9 us
    ppermute x15, starting transfers between devices, move(): return lax.ppermute(value, 'pts', pairs)  11.1 us
    ppermute x2, waiting for transfers between devices, local_pair(): returned.append(lax.ppermute(sent, 'ka', swap))  9.87 us
    pallas_call x2, Pallas kernels, convolve(): pl.pallas_call(kernel, out_shape=(jax.ShapeDtypeStruct((count, 2, 2 * row...  8.97 us
    pallas_call x2, Pallas kernels, coulomb_transform(): pl.pallas_call(kernel, out_shape=jax.ShapeDtypeStruct(shape, jnp.float32)...  6.49 us
    ppermute x3, starting transfers between devices, local_pair(): other[i].append(lax.ppermute(value, 'ka', swap))  3.65 us
    unnamed x42, local copies, waits for them, and re-layouts  3.18 us
  transfers between devices with their start and end apart: 21, of which 9 were waited for; matrix products, arithmetic and copies ran while one was open for 3% of the time, Pallas kernels for 43%

profile of v1, /device:TPU:0, one launch (start us, length us, event | category | flops | bytes accessed | tf_op | source)
XLA Modules:
  0.0 94.2 jit_solution(9484337512723911801)
XLA Ops:
  0.0 1.5 %slice.21 = bf16[108,2,1,384]{3,2,1,0:T(2,128)(2,1)S(1)} slice(bf16[108,2,256,384]{3,2,1,0:T(8,128)(2,1)} %refs_16_.3), slice={[0:108], [0:2], [0:1], [0:384]} | slice | bytes 331776 | tf_op jit(solution)/shard_map/slice | solution.py:402
  2.7 3.1 %collective-permute-start.9 = (bf16[112,640]{1,0:T(8,128)(2,1)S(1)}, bf16[112,640]{1,0:T(8,128)(2,1)S(1)}, u32[]{:S(2)}, u32[]{:S(2)}) collective-permute-start(bf16[112,640]{1,0:T(8,128)(2,1)S(1)} %fusion.7.refs_0_), channel_id=1, source_target_pairs={{0,2},{1,3},{2,0},{3,1},{4,6},{5,7},{6,4},{7,5},{8,10},{9,11},{10,... | collective-permute-start | bytes 430088 | tf_op jit(solution)/shard_map/ppermute | solution.py:426
  5.8 1.5 %collective-permute-start.5 = (bf16[112,640]{1,0:T(8,128)(2,1)S(1)}, bf16[112,640]{1,0:T(8,128)(2,1)S(1)}, u32[]{:S(2)}, u32[]{:S(2)}) collective-permute-start(bf16[112,640]{1,0:T(8,128)(2,1)S(1)} %fusion.7.refs_0_), channel_id=1, source_target_pairs={{0,6},{1,15},{2,4},{3,13},{4,10},{5,3},{6,8},{7,1},{8,14},{9,7},{1... | collective-permute-start | bytes 430088 | tf_op jit(solution)/shard_map/ppermute | solution.py:426
  7.3 1.6 %collective-permute-start.1 = (bf16[112,640]{1,0:T(8,128)(2,1)S(1)}, bf16[112,640]{1,0:T(8,128)(2,1)S(1)}, u32[]{:S(2)}, u32[]{:S(2)}) collective-permute-start(bf16[112,640]{1,0:T(8,128)(2,1)S(1)} %fusion.7.refs_0_), channel_id=1, source_target_pairs={{0,4},{1,13},{2,6},{3,15},{4,8},{5,1},{6,10},{7,3},{8,12},{9,5},{1... | collective-permute-start | bytes 430088 | tf_op jit(solution)/shard_map/ppermute | solution.py:426
  10.0 1.1 %collective-permute-done.9.refs_10_ = bf16[112,640]{1,0:T(8,128)(2,1)S(1)} collective-permute-done((bf16[112,640]{1,0:T(8,128)(2,1)S(1)}, bf16[112,640]{1,0:T(8,128)(2,1)S(1)}, u32[]{:S(2)}, u32[]{:S(2)}) %collective-permute-start.9) | collective-permute-done | bytes 143392 | tf_op jit(solution)/shard_map/ppermute | solution.py:426
  11.1 4.0 %collective-permute-done.5.refs_6_ = bf16[112,640]{1,0:T(8,128)(2,1)S(1)} collective-permute-done((bf16[112,640]{1,0:T(8,128)(2,1)S(1)}, bf16[112,640]{1,0:T(8,128)(2,1)S(1)}, u32[]{:S(2)}, u32[]{:S(2)}) %collective-permute-start.5) | collective-permute-done | bytes 143392 | tf_op jit(solution)/shard_map/ppermute | solution.py:426
  15.2 1.8 %collective-permute-start.6 = (bf16[112,640]{1,0:T(8,128)(2,1)S(1)}, bf16[112,640]{1,0:T(8,128)(2,1)S(1)}, u32[]{:S(2)}, u32[]{:S(2)}) collective-permute-start(bf16[112,640]{1,0:T(8,128)(2,1)S(1)} %collective-permute-done.5.refs_6_), channel_id=1, source_target_pairs={{0,1},{1,0},{2,3},{3,2},{4,5},{5,4},{6,7},{7,6},{8,9},{9,8},{10,11... | collective-permute-start | bytes 430088 | tf_op jit(solution)/shard_map/ppermute | solution.py:426
  17.0 2.3 %collective-permute-start.2 = (bf16[112,640]{1,0:T(8,128)(2,1)S(1)}, bf16[112,640]{1,0:T(8,128)(2,1)S(1)}, u32[]{:S(2)}, u32[]{:S(2)}) collective-permute-start(bf16[112,640]{1,0:T(8,128)(2,1)S(1)} %collective-permute-done.1.refs_2_), channel_id=1, source_target_pairs={{0,1},{1,0},{2,3},{3,2},{4,5},{5,4},{6,7},{7,6},{8,9},{9,8},{10,11... | collective-permute-start | bytes 430088 | tf_op jit(solution)/shard_map/ppermute | solution.py:426
  19.6 3.9 %collective-permute-done.13.refs_14_ = bf16[112,640]{1,0:T(8,128)(2,1)S(1)} collective-permute-done((bf16[112,640]{1,0:T(8,128)(2,1)S(1)}, bf16[112,640]{1,0:T(8,128)(2,1)S(1)}, u32[]{:S(2)}, u32[]{:S(2)}) %collective-permute-start.13) | collective-permute-done | bytes 143392 | tf_op jit(solution)/shard_map/ppermute | solution.py:426
  23.6 2.1 %take_rows.1 = bf16[108,2,8,256]{3,2,1,0:T(8,128)(2,1)} custom-call(s32[1]{0:T(128)S(6)} %sub.66.which_ref, bf16[108,2,16,256]{3,2,1,0:T(8,128)(2,1)} %own_ref.3), custom_call_target="tpu_custom_call" | custom-call | tf_op jit(solution)/shard_map/take_rows/pallas_call | solution.py:161
  25.9 1.6 %collective-permute-start.17 = (bf16[108,2,8,256]{3,2,1,0:T(8,128)(2,1)}, bf16[108,2,8,256]{3,2,1,0:T(8,128)(2,1)S(1)}, u32[]{:S(2)}, u32[]{:S(2)}) collective-permute-start(bf16[108,2,8,256]{3,2,1,0:T(8,128)(2,1)} %take_rows.1), channel_id=1, source_target_pairs={{0,16},{16,0},{1,17},{17,1},{2,18},{18,2},{3,19},{19,3},{4,20},{20... | collective-permute-start | bytes 2654216 | tf_op jit(solution)/shard_map/ppermute | solution.py:493
  27.9 1.6 %collective-permute-done.7.refs_8_ = bf16[112,640]{1,0:T(8,128)(2,1)S(1)} collective-permute-done((bf16[112,640]{1,0:T(8,128)(2,1)S(1)}, bf16[112,640]{1,0:T(8,128)(2,1)S(1)}, u32[]{:S(2)}, u32[]{:S(2)}) %collective-permute-start.7) | collective-permute-done | bytes 143392 | tf_op jit(solution)/shard_map/ppermute | solution.py:426
  29.5 1.7 %collective-permute-done.3.refs_4_ = bf16[112,640]{1,0:T(8,128)(2,1)S(1)} collective-permute-done((bf16[112,640]{1,0:T(8,128)(2,1)S(1)}, bf16[112,640]{1,0:T(8,128)(2,1)S(1)}, u32[]{:S(2)}, u32[]{:S(2)}) %collective-permute-start.3) | collective-permute-done | bytes 143392 | tf_op jit(solution)/shard_map/ppermute | solution.py:426
  33.3 14.0 %density_part.2 = (bf16[72,2,8,256]{3,2,1,0:T(8,128)(2,1)}, bf16[72,2,8,256]{3,2,1,0:T(8,128)(2,1)}) custom-call(s32[108]{0:T(128)} %get-tuple-element.17.order_ref, s32[108]{0:T(128)} %get-tuple-element.18.tiles_ref, bf16[256,256]{1,0:T(8,128)(2,1)} %and_convert_fusion.spread_ref, bf16[112,640]{1,0:T(8,128)(2,1)} %copy-done.2, bf16[112,640]{1,0:T(8,128)(2,1)} %copy-done.6, ...), custom_call_target="tpu_custom_call" | custom-call | tf_op jit(solution)/shard_map/density_part/pallas_call | solution.py:117
  47.3 1.6 %collective-permute-start.15 = (bf16[72,2,8,256]{3,2,1,0:T(8,128)(2,1)}, bf16[72,2,8,256]{3,2,1,0:T(8,128)(2,1)S(1)}, u32[]{:S(2)}, u32[]{:S(2)}) collective-permute-start(bf16[72,2,8,256]{3,2,1,0:T(8,128)(2,1)} %get-tuple-element.22), channel_id=1, source_target_pairs={{0,16},{16,0},{1,17},{17,1},{2,18},{18,2},{3,19},{19,3},{4,20},{20... | collective-permute-start | bytes 1769480 | tf_op jit(solution)/shard_map/ppermute | solution.py:512
  48.9 9.4 %density_part.3 = (bf16[36,2,8,256]{3,2,1,0:T(8,128)(2,1)}, bf16[36,2,8,128]{3,2,1,0:T(8,128)(2,1)}, bf16[36,2,8,128]{3,2,1,0:T(8,128)(2,1)}) custom-call(s32[108]{0:T(128)} %get-tuple-element.17.order_ref, s32[108]{0:T(128)} %get-tuple-element.18.tiles_ref, bf16[256,256]{1,0:T(8,128)(2,1)} %and_convert_fusion.spread_ref, bf16[112,640]{1,0:T(8,128)(2,1)} %copy-done.2, ...), custom_call_target="tpu_custom_call" | custom-call | tf_op jit(solution)/shard_map/density_part/pallas_call | solution.py:117
  58.5 1.8 %collective-permute-start.16 = (bf16[36,2,8,128]{3,2,1,0:T(8,128)(2,1)}, bf16[36,2,8,128]{3,2,1,0:T(8,128)(2,1)S(1)}, u32[]{:S(2)}, u32[]{:S(2)}) collective-permute-start(bf16[36,2,8,128]{3,2,1,0:T(8,128)(2,1)} %get-tuple-element.23), channel_id=1, source_target_pairs={{0,16},{16,0},{1,17},{17,1},{2,18},{18,2},{3,19},{19,3},{4,20},{20... | collective-permute-start | bytes 442376 | tf_op jit(solution)/shard_map/ppermute | solution.py:512
  61.2 3.2 %coulomb_transform.3.refs_4_ = f32[2,6,3,6,2,8,128]{6,5,4,3,2,1,0:T(8,128)} custom-call(s32[1]{0:T(128)} %bitcast.which_ref, bf16[108,2,16,256]{3,2,1,0:T(8,128)(2,1)} %own_ref.3, bf16[108,2,8,256]{3,2,1,0:T(8,128)(2,1)} %copy-done), custom_call_target="tpu_custom_call" | custom-call | tf_op jit(solution)/shard_map/coulomb_transform/pallas_call | solution.py:260
  64.5 2.5 %collective-permute-done.18.refs_3_ = bf16[36,2,8,128]{3,2,1,0:T(8,128)(2,1)S(1)} collective-permute-done((bf16[36,2,8,128]{3,2,1,0:T(8,128)(2,1)}, bf16[36,2,8,128]{3,2,1,0:T(8,128)(2,1)S(1)}, u32[]{:S(2)}, u32[]{:S(2)}) %collective-permute-start.18) | collective-permute-done | bytes 147488 | tf_op jit(solution)/shard_map/ppermute | solution.py:512
  67.8 4.5 %convolve.2 = (bf16[108,2,16,256]{3,2,1,0:T(8,128)(2,1)}, bf16[108,2,8,128]{3,2,1,0:T(8,128)(2,1)}) custom-call(s32[1]{0:T(128)} %bitcast.which_ref, bf16[72,2,8,256]{3,2,1,0:T(8,128)(2,1)} %get-tuple-element.20.refs_0_, bf16[36,2,8,256]{3,2,1,0:T(8,128)(2,1)} %get-tuple-element.21.refs_1_, bf16[72,2,8,256]{3,2,1,0:T(8,128)(2,1)} %copy-done.1, ...), custom_call_target="tpu_custom_call" | custom-call | tf_op jit(solution)/shard_map/convolve/pallas_call | solution.py:334
  72.3 1.5 %collective-permute-start.19 = (bf16[108,2,8,128]{3,2,1,0:T(8,128)(2,1)}, bf16[108,2,8,128]{3,2,1,0:T(8,128)(2,1)S(1)}, u32[]{:S(2)}, u32[]{:S(2)}) collective-permute-start(bf16[108,2,8,128]{3,2,1,0:T(8,128)(2,1)} %get-tuple-element.27), channel_id=1, source_target_pairs={{0,16},{16,0},{1,17},{17,1},{2,18},{18,2},{3,19},{19,3},{4,20},{20... | collective-permute-start | bytes 1327112 | tf_op jit(solution)/shard_map/ppermute | solution.py:519
  73.8 3.2 %coulomb_transform.2.refs_4_ = f32[2,6,3,6,2,8,128]{6,5,4,3,2,1,0:T(8,128)} custom-call(s32[1]{0:T(128)} %bitcast.which_ref, bf16[108,2,16,256]{3,2,1,0:T(8,128)(2,1)} %own_ref.3, bf16[108,2,8,256]{3,2,1,0:T(8,128)(2,1)} %copy-done), custom_call_target="tpu_custom_call" | custom-call | tf_op jit(solution)/shard_map/coulomb_transform/pallas_call | solution.py:260
  77.7 4.5 %convolve.3 = (bf16[108,2,16,256]{3,2,1,0:T(8,128)(2,1)}, bf16[108,2,8,128]{3,2,1,0:T(8,128)(2,1)}) custom-call(s32[1]{0:T(128)} %bitcast.which_ref, bf16[72,2,8,256]{3,2,1,0:T(8,128)(2,1)} %get-tuple-element.20.refs_0_, bf16[36,2,8,256]{3,2,1,0:T(8,128)(2,1)} %get-tuple-element.21.refs_1_, ...), custom_call_target="tpu_custom_call", output_to_operand_aliasing={{0}: (6, {})} | custom-call | tf_op jit(solution)/shard_map/convolve/pallas_call | solution.py:334
  84.5 8.8 %collective-permute-done.20 = bf16[108,2,8,128]{3,2,1,0:T(8,128)(2,1)S(1)} collective-permute-done((bf16[108,2,8,128]{3,2,1,0:T(8,128)(2,1)}, bf16[108,2,8,128]{3,2,1,0:T(8,128)(2,1)S(1)}, u32[]{:S(2)}, u32[]{:S(2)}) %collective-permute-start.20) | collective-permute-done | bytes 442400 | tf_op jit(solution)/shard_map/ppermute | solution.py:519
  (89 shorter events, 11.3 us)
Async XLA Ops:
  2.7 29.8 %copy-start.2 = (bf16[112,640]{1,0:T(8,128)(2,1)}, bf16[112,640]{1,0:T(8,128)(2,1)S(1)}, u32[]{:S(2)}) copy-start(bf16[112,640]{1,0:T(8,128)(2,1)S(1)} %fusion.7.refs_0_) | copy-start | bytes 430084
  2.7 8.4 %collective-permute-start.9 = (bf16[112,640]{1,0:T(8,128)(2,1)S(1)}, bf16[112,640]{1,0:T(8,128)(2,1)S(1)}, u32[]{:S(2)}, u32[]{:S(2)}) collective-permute-start(bf16[112,640]{1,0:T(8,128)(2,1)S(1)} %fusion.7.refs_0_), channel_id=1, source_target_pairs={{0,2},{1,3},{2,0},{3,1},{4,6},{5,7},{6,4},{7,5},{8,10},{9,11},{10,... | collective-permute-start | bytes 430088 | tf_op jit(solution)/shard_map/ppermute | solution.py:426
  5.8 9.3 %collective-permute-start.5 = (bf16[112,640]{1,0:T(8,128)(2,1)S(1)}, bf16[112,640]{1,0:T(8,128)(2,1)S(1)}, u32[]{:S(2)}, u32[]{:S(2)}) collective-permute-start(bf16[112,640]{1,0:T(8,128)(2,1)S(1)} %fusion.7.refs_0_), channel_id=1, source_target_pairs={{0,6},{1,15},{2,4},{3,13},{4,10},{5,3},{6,8},{7,1},{8,14},{9,7},{1... | collective-permute-start | bytes 430088 | tf_op jit(solution)/shard_map/ppermute | solution.py:426
  7.3 9.6 %collective-permute-start.1 = (bf16[112,640]{1,0:T(8,128)(2,1)S(1)}, bf16[112,640]{1,0:T(8,128)(2,1)S(1)}, u32[]{:S(2)}, u32[]{:S(2)}) collective-permute-start(bf16[112,640]{1,0:T(8,128)(2,1)S(1)} %fusion.7.refs_0_), channel_id=1, source_target_pairs={{0,4},{1,13},{2,6},{3,15},{4,8},{5,1},{6,10},{7,3},{8,12},{9,5},{1... | collective-permute-start | bytes 430088 | tf_op jit(solution)/shard_map/ppermute | solution.py:426
  8.9 8.1 %collective-permute-start = (bf16[112,640]{1,0:T(8,128)(2,1)S(1)}, bf16[112,640]{1,0:T(8,128)(2,1)S(1)}, u32[]{:S(2)}, u32[]{:S(2)}) collective-permute-start(bf16[112,640]{1,0:T(8,128)(2,1)S(1)} %fusion.7.refs_0_), channel_id=1, source_target_pairs={{0,1},{1,0},{2,3},{3,2},{4,5},{5,4},{6,7},{7,6},{8,9},{9,8},{10,11... | collective-permute-start | bytes 430088 | tf_op jit(solution)/shard_map/ppermute | solution.py:426
  11.1 21.4 %copy-start.3 = (bf16[112,640]{1,0:T(8,128)(2,1)}, bf16[112,640]{1,0:T(8,128)(2,1)S(1)}, u32[]{:S(2)}) copy-start(bf16[112,640]{1,0:T(8,128)(2,1)S(1)} %collective-permute-done.9.refs_10_) | copy-start | bytes 430084
  11.1 8.2 %collective-permute-start.10 = (bf16[112,640]{1,0:T(8,128)(2,1)S(1)}, bf16[112,640]{1,0:T(8,128)(2,1)S(1)}, u32[]{:S(2)}, u32[]{:S(2)}) collective-permute-start(bf16[112,640]{1,0:T(8,128)(2,1)S(1)} %collective-permute-done.9.refs_10_), channel_id=1, source_target_pairs={{0,1},{1,0},{2,3},{3,2},{4,5},{5,4},{6,7},{7,6},{8,9},{9,8},{10,11... | collective-permute-start | bytes 430088 | tf_op jit(solution)/shard_map/ppermute | solution.py:426
  15.1 17.4 %copy-start.4 = (bf16[112,640]{1,0:T(8,128)(2,1)}, bf16[112,640]{1,0:T(8,128)(2,1)S(1)}, u32[]{:S(2)}) copy-start(bf16[112,640]{1,0:T(8,128)(2,1)S(1)} %collective-permute-done.5.refs_6_) | copy-start | bytes 430084
  15.1 8.4 %collective-permute-start.13 = (bf16[112,640]{1,0:T(8,128)(2,1)S(1)}, bf16[112,640]{1,0:T(8,128)(2,1)S(1)}, u32[]{:S(2)}, u32[]{:S(2)}) collective-permute-start(bf16[112,640]{1,0:T(8,128)(2,1)S(1)} %collective-permute-done.5.refs_6_), channel_id=1, source_target_pairs={{0,4},{1,13},{2,6},{3,15},{4,8},{5,1},{6,10},{7,3},{8,12},{9,5},{1... | collective-permute-start | bytes 430088 | tf_op jit(solution)/shard_map/ppermute | solution.py:426
  15.2 10.7 %collective-permute-start.6 = (bf16[112,640]{1,0:T(8,128)(2,1)S(1)}, bf16[112,640]{1,0:T(8,128)(2,1)S(1)}, u32[]{:S(2)}, u32[]{:S(2)}) collective-permute-start(bf16[112,640]{1,0:T(8,128)(2,1)S(1)} %collective-permute-done.5.refs_6_), channel_id=1, source_target_pairs={{0,1},{1,0},{2,3},{3,2},{4,5},{5,4},{6,7},{7,6},{8,9},{9,8},{10,11... | collective-permute-start | bytes 430088 | tf_op jit(solution)/shard_map/ppermute | solution.py:426
  17.0 10.5 %collective-permute-start.11 = (bf16[112,640]{1,0:T(8,128)(2,1)S(1)}, bf16[112,640]{1,0:T(8,128)(2,1)S(1)}, u32[]{:S(2)}, u32[]{:S(2)}) collective-permute-start(bf16[112,640]{1,0:T(8,128)(2,1)S(1)} %collective-permute-done.1.refs_2_), channel_id=1, source_target_pairs={{0,4},{1,13},{2,6},{3,15},{4,8},{5,1},{6,10},{7,3},{8,12},{9,5},{1... | collective-permute-start | bytes 430088 | tf_op jit(solution)/shard_map/ppermute | solution.py:426
  17.0 10.7 %collective-permute-start.2 = (bf16[112,640]{1,0:T(8,128)(2,1)S(1)}, bf16[112,640]{1,0:T(8,128)(2,1)S(1)}, u32[]{:S(2)}, u32[]{:S(2)}) collective-permute-start(bf16[112,640]{1,0:T(8,128)(2,1)S(1)} %collective-permute-done.1.refs_2_), channel_id=1, source_target_pairs={{0,1},{1,0},{2,3},{3,2},{4,5},{5,4},{6,7},{7,6},{8,9},{9,8},{10,11... | collective-permute-start | bytes 430088 | tf_op jit(solution)/shard_map/ppermute | solution.py:426
  19.3 10.2 %collective-permute-start.7 = (bf16[112,640]{1,0:T(8,128)(2,1)S(1)}, bf16[112,640]{1,0:T(8,128)(2,1)S(1)}, u32[]{:S(2)}, u32[]{:S(2)}) collective-permute-start(bf16[112,640]{1,0:T(8,128)(2,1)S(1)} %collective-permute-done.refs_1_), channel_id=1, source_target_pairs={{0,6},{1,15},{2,4},{3,13},{4,10},{5,3},{6,8},{7,1},{8,14},{9,7},{1... | collective-permute-start | bytes 430088 | tf_op jit(solution)/shard_map/ppermute | solution.py:426
  23.6 7.6 %collective-permute-start.3 = (bf16[112,640]{1,0:T(8,128)(2,1)S(1)}, bf16[112,640]{1,0:T(8,128)(2,1)S(1)}, u32[]{:S(2)}, u32[]{:S(2)}) collective-permute-start(bf16[112,640]{1,0:T(8,128)(2,1)S(1)} %collective-permute-done.refs_1_), channel_id=1, source_target_pairs={{0,4},{1,13},{2,6},{3,15},{4,8},{5,1},{6,10},{7,3},{8,12},{9,5},{1... | collective-permute-start | bytes 430088 | tf_op jit(solution)/shard_map/ppermute | solution.py:426
  25.9 34.5 %collective-permute-start.17 = (bf16[108,2,8,256]{3,2,1,0:T(8,128)(2,1)}, bf16[108,2,8,256]{3,2,1,0:T(8,128)(2,1)S(1)}, u32[]{:S(2)}, u32[]{:S(2)}) collective-permute-start(bf16[108,2,8,256]{3,2,1,0:T(8,128)(2,1)} %take_rows.1), channel_id=1, source_target_pairs={{0,16},{16,0},{1,17},{17,1},{2,18},{18,2},{3,19},{19,3},{4,20},{20... | collective-permute-start | bytes 2654216 | tf_op jit(solution)/shard_map/ppermute | solution.py:493
  27.4 4.5 %collective-permute-start.14 = (bf16[112,640]{1,0:T(8,128)(2,1)S(1)}, bf16[112,640]{1,0:T(8,128)(2,1)S(1)}, u32[]{:S(2)}, u32[]{:S(2)}) collective-permute-start(bf16[112,640]{1,0:T(8,128)(2,1)S(1)} %collective-permute-done.13.refs_14_), channel_id=1, source_target_pairs={{0,1},{1,0},{2,3},{3,2},{4,5},{5,4},{6,7},{7,6},{8,9},{9,8},{10,11... | collective-permute-start | bytes 430088 | tf_op jit(solution)/shard_map/ppermute | solution.py:426
  27.7 4.2 %collective-permute-start.12 = (bf16[112,640]{1,0:T(8,128)(2,1)S(1)}, bf16[112,640]{1,0:T(8,128)(2,1)S(1)}, u32[]{:S(2)}, u32[]{:S(2)}) collective-permute-start(bf16[112,640]{1,0:T(8,128)(2,1)S(1)} %collective-permute-done.11.refs_12_), channel_id=1, source_target_pairs={{0,1},{1,0},{2,3},{3,2},{4,5},{5,4},{6,7},{7,6},{8,9},{9,8},{10,11... | collective-permute-start | bytes 430088 | tf_op jit(solution)/shard_map/ppermute | solution.py:426
  29.5 2.4 %collective-permute-start.8 = (bf16[112,640]{1,0:T(8,128)(2,1)S(1)}, bf16[112,640]{1,0:T(8,128)(2,1)S(1)}, u32[]{:S(2)}, u32[]{:S(2)}) collective-permute-start(bf16[112,640]{1,0:T(8,128)(2,1)S(1)} %collective-permute-done.7.refs_8_), channel_id=1, source_target_pairs={{0,1},{1,0},{2,3},{3,2},{4,5},{5,4},{6,7},{7,6},{8,9},{9,8},{10,11... | collective-permute-start | bytes 430088 | tf_op jit(solution)/shard_map/ppermute | solution.py:426
  31.2 1.4 %collective-permute-start.4 = (bf16[112,640]{1,0:T(8,128)(2,1)S(1)}, bf16[112,640]{1,0:T(8,128)(2,1)S(1)}, u32[]{:S(2)}, u32[]{:S(2)}) collective-permute-start(bf16[112,640]{1,0:T(8,128)(2,1)S(1)} %collective-permute-done.3.refs_4_), channel_id=1, source_target_pairs={{0,1},{1,0},{2,3},{3,2},{4,5},{5,4},{6,7},{7,6},{8,9},{9,8},{10,11... | collective-permute-start | bytes 430088 | tf_op jit(solution)/shard_map/ppermute | solution.py:426
  47.3 19.6 %collective-permute-start.15 = (bf16[72,2,8,256]{3,2,1,0:T(8,128)(2,1)}, bf16[72,2,8,256]{3,2,1,0:T(8,128)(2,1)S(1)}, u32[]{:S(2)}, u32[]{:S(2)}) collective-permute-start(bf16[72,2,8,256]{3,2,1,0:T(8,128)(2,1)} %get-tuple-element.22), channel_id=1, source_target_pairs={{0,16},{16,0},{1,17},{17,1},{2,18},{18,2},{3,19},{19,3},{4,20},{20... | collective-permute-start | bytes 1769480 | tf_op jit(solution)/shard_map/ppermute | solution.py:512
  58.2 8.7 %collective-permute-start.18 = (bf16[36,2,8,128]{3,2,1,0:T(8,128)(2,1)}, bf16[36,2,8,128]{3,2,1,0:T(8,128)(2,1)S(1)}, u32[]{:S(2)}, u32[]{:S(2)}) collective-permute-start(bf16[36,2,8,128]{3,2,1,0:T(8,128)(2,1)} %get-tuple-element.24), channel_id=1, source_target_pairs={{0,16},{16,0},{1,17},{17,1},{2,18},{18,2},{3,19},{19,3},{4,20},{20... | collective-permute-start | bytes 442376 | tf_op jit(solution)/shard_map/ppermute | solution.py:512
  58.5 18.5 %collective-permute-start.16 = (bf16[36,2,8,128]{3,2,1,0:T(8,128)(2,1)}, bf16[36,2,8,128]{3,2,1,0:T(8,128)(2,1)S(1)}, u32[]{:S(2)}, u32[]{:S(2)}) collective-permute-start(bf16[36,2,8,128]{3,2,1,0:T(8,128)(2,1)} %get-tuple-element.23), channel_id=1, source_target_pairs={{0,16},{16,0},{1,17},{17,1},{2,18},{18,2},{3,19},{19,3},{4,20},{20... | collective-permute-start | bytes 442376 | tf_op jit(solution)/shard_map/ppermute | solution.py:512
  72.3 11.5 %collective-permute-start.19 = (bf16[108,2,8,128]{3,2,1,0:T(8,128)(2,1)}, bf16[108,2,8,128]{3,2,1,0:T(8,128)(2,1)S(1)}, u32[]{:S(2)}, u32[]{:S(2)}) collective-permute-start(bf16[108,2,8,128]{3,2,1,0:T(8,128)(2,1)} %get-tuple-element.27), channel_id=1, source_target_pairs={{0,16},{16,0},{1,17},{17,1},{2,18},{18,2},{3,19},{19,3},{4,20},{20... | collective-permute-start | bytes 1327112 | tf_op jit(solution)/shard_map/ppermute | solution.py:519
  82.2 11.2 %collective-permute-start.20 = (bf16[108,2,8,128]{3,2,1,0:T(8,128)(2,1)}, bf16[108,2,8,128]{3,2,1,0:T(8,128)(2,1)S(1)}, u32[]{:S(2)}, u32[]{:S(2)}) collective-permute-start(bf16[108,2,8,128]{3,2,1,0:T(8,128)(2,1)} %get-tuple-element.28), channel_id=1, source_target_pairs={{0,16},{16,0},{1,17},{17,1},{2,18},{18,2},{3,19},{19,3},{4,20},{20... | collective-permute-start | bytes 1327112 | tf_op jit(solution)/shard_map/ppermute | solution.py:519
  (18 other events, 96.0 us)
